TPU v7x, 512 devices: a whole 4x8x8 slice. The times are simulated.
512 devices in a mesh: sub: 64 (over y, z), crow: 4 (over x_lo, core), ccol: 2 (over x_hi).
Axes of the slice: x: 4 (x_hi: 2, x_lo: 2; x = x_hi * 2 + x_lo), y: 8, z: 8, core: 2. Of those that a mesh axis runs over, the one named last changes fastest.
Arguments:
- loads: bfloat16 [128, 1024, 128], P('sub'), may hold values from -6 to 6
- stiffness: bfloat16 [128, 1024, 1024], P('sub', ('crow', 'ccol'))
- local_inverse: bfloat16 [128, 1024, 1024], P('sub', ('crow', 'ccol'))
- coarse_basis: bfloat16 [128, 1024, 48], P('sub', ('crow', 'ccol')), may hold values from -0.1875 to 0.1875
- coarse_inverse: bfloat16 [6144, 6144], P('sub', ('crow', 'ccol'))
- coarse_index: int32 [128, 48], P('sub'), may hold values from 0 to 6143, as said below
- left_rows: int32 [128, 128], P('sub'), may hold values from 0 to 1023, as said below
- right_rows: int32 [128, 128], P('sub'), may hold values from 0 to 1023, as said below
Outputs:
- second_pass: float32 [128, 1024, 128], P('sub', ('crow', 'ccol'))
- final_residual: float32 [128, 1024, 128], P('sub', ('crow', 'ccol'))
Inputs may be any that keep to these rules, and one draw needn't show every extreme that they name: `coarse_index`: every value 0 to 6143 appears exactly once in the whole array. Of the 96 values in the rows of one index of sub, at most 24 lie in one block of 768 consecutive coarse rows starting at a multiple of 768, and that most is reached. In each subdomain the 128 entries of left_rows and the 128 entries of right_rows are 256 distinct rows. `right_rows`: see left_rows.
All inputs are finite; a program needn't handle non-finite values.
Results may differ from a plain program's by a relative error of at most 0.0067.
Values may be sent and summed in bfloat16 or wider, within the bound.
A program may use at most 64 MiB of HBM per device.

v0:
```python
import jax
import jax.numpy as jnp
from jax import lax
from jax.sharding import PartitionSpec as P


def padded(block, sides, width):
    for axis, dim in sides:
        count = lax.axis_size(axis)
        forward = [(i, i + 1) for i in range(count - 1)]
        forward.append((count - 1, 0))
        backward = [(target, source) for source, target in forward]
        low = lax.ppermute(
            lax.slice_in_dim(block, block.shape[dim] - width, None, axis=dim), axis, forward
        )
        high = lax.ppermute(lax.slice_in_dim(block, 0, width, axis=dim), axis, backward)
        block = jnp.concatenate([low, block, high], axis=dim)
    return block


def fold_product(matrix, gathered_piece):
    return jnp.einsum("sij,sjc->sic", matrix, gathered_piece, preferred_element_type=jnp.float32)


def apply_stiffness(iterate, stiffness, pick_left, pick_right):
    sub_count, row_count, case_count = iterate.shape
    rounded = iterate.astype(jnp.bfloat16)
    product = fold_product(stiffness, lax.all_gather(rounded, ("crow", "ccol"), axis=1, tiled=True))
    product_b = product.astype(jnp.bfloat16)
    left_part = jnp.einsum("sfi,sic->sfc", pick_left, product_b, preferred_element_type=jnp.float32)
    right_part = jnp.einsum(
        "sfi,sic->sfc", pick_right, product_b, preferred_element_type=jnp.float32
    )
    partial_faces = jnp.stack([left_part, right_part], axis=1)
    boundary = lax.psum(partial_faces.astype(jnp.bfloat16), ("crow", "ccol"))
    extended = padded(boundary, (("sub", 0),), 1)
    from_before = extended[:sub_count, 1]
    from_after = extended[2:, 0]
    added_left = jnp.einsum(
        "sfi,sfc->sic", pick_left, from_before, preferred_element_type=jnp.float32
    )
    added_right = jnp.einsum(
        "sfi,sfc->sic", pick_right, from_after, preferred_element_type=jnp.float32
    )
    return product_b.astype(jnp.float32) + added_left + added_right


def coarse_step(restricted, coarse_inverse, coarse_index):
    sub_count, mode_count, case_count = restricted.shape
    flat_rows = restricted.reshape(sub_count * mode_count, case_count)
    flat_index = coarse_index.reshape(-1)
    owned_rows, block_width = coarse_inverse.shape
    block_index = lax.axis_index(("crow", "ccol"))
    arrived, arrived_index = (
        lax.all_gather(flat_rows, "sub", axis=0, tiled=True),
        lax.all_gather(flat_index, "sub", axis=0, tiled=True),
    )
    shifted_place = arrived_index - block_index * block_width
    inside = (shifted_place >= 0) & (shifted_place < block_width)
    arrived_place = jnp.where(inside, shifted_place, block_width)
    ordered = (
        jnp.zeros((block_width + 1, case_count), jnp.bfloat16)
        .at[arrived_place]
        .set(arrived)[:block_width]
    )
    partial_coarse = jnp.dot(coarse_inverse, ordered, preferred_element_type=jnp.float32)
    coarse = lax.psum(partial_coarse, ("crow", "ccol")).astype(jnp.bfloat16)
    everything = lax.all_gather(coarse, "sub", axis=0, tiled=True)
    picked = everything[flat_index]
    return picked.reshape(sub_count, mode_count, case_count)


def precondition(local_part, residual_rows, coarse_basis, coarse_inverse, coarse_index):
    partial_modes = jnp.einsum(
        "sik,sic->skc", coarse_basis, residual_rows, preferred_element_type=jnp.float32
    )
    restricted = lax.psum(partial_modes, ("crow", "ccol")).astype(jnp.bfloat16)
    picked = coarse_step(restricted, coarse_inverse, coarse_index)
    return local_part + jnp.einsum(
        "sik,skc->sic", coarse_basis, picked, preferred_element_type=jnp.float32
    )


def body(
    loads,
    stiffness,
    local_inverse,
    coarse_basis,
    coarse_inverse,
    coarse_index,
    left_rows,
    right_rows,
):
    sub_count, row_count, iface_count = stiffness.shape
    group_index = lax.axis_index(("crow", "ccol"))
    first_row = group_index * row_count
    loads_rows = lax.dynamic_slice_in_dim(loads, first_row, row_count, 1)
    local_rows = first_row + jnp.arange(row_count, dtype=jnp.int32)
    pick_left = (left_rows[:, :, None] == local_rows[None, None, :]).astype(jnp.bfloat16)
    pick_right = (right_rows[:, :, None] == local_rows[None, None, :]).astype(jnp.bfloat16)
    first_local = jnp.einsum(
        "sij,sjc->sic", local_inverse, loads, preferred_element_type=jnp.float32
    )
    first_pass = precondition(first_local, loads_rows, coarse_basis, coarse_inverse, coarse_index)
    image_first = apply_stiffness(first_pass, stiffness, pick_left, pick_right)
    residual_b = (loads_rows.astype(jnp.float32) - image_first).astype(jnp.bfloat16)
    second_local = fold_product(
        local_inverse, lax.all_gather(residual_b, ("crow", "ccol"), axis=1, tiled=True)
    )
    second_pass = first_pass + precondition(
        second_local, residual_b, coarse_basis, coarse_inverse, coarse_index
    )
    image_second = apply_stiffness(second_pass, stiffness, pick_left, pick_right)
    final_residual = loads_rows.astype(jnp.float32) - image_second
    return (second_pass, final_residual)


def solution(mesh):
    return jax.shard_map(
        body,
        mesh=mesh,
        in_specs=(
            P("sub", None, None),
            P("sub", ("crow", "ccol"), None),
            P("sub", ("crow", "ccol"), None),
            P("sub", ("crow", "ccol"), None),
            P("sub", ("crow", "ccol")),
            P("sub", None),
            P("sub", None),
            P("sub", None),
        ),
        out_specs=(P("sub", ("crow", "ccol"), None), P("sub", ("crow", "ccol"), None)),
        check_vma=False,
    )
```

profile of v0, /device:TPU:6, one launch (start us, length us, event | category | flops | bytes accessed | tf_op | source)
XLA Modules:
  0.0 929.7 jit_solution(8455041256860478172)
XLA Ops:
  7.2 0.0 all-gather.5.cloned.1.call-start
  7.2 1.1 convolution_bitcast_fusion.4
  8.3 34.2 %psum.42 = bf16[2,48,128]{2,1,0:T(8,128)(2,1)} all-reduce(f32[2,48,128]{2,1,0:T(8,128)S(1)} %convolution_bitcast_fusion.4), channel_id=1, replica_groups=mesh['sub'=64,'crow'=4,'ccol'=2] {'crow','ccol'}, use_global_device_ids=true, to_apply=%region_0.0 | all-reduce | flops 12288 | bytes 73728 | tf_op jit(solution)/shard_map/psum | solution.py:77
  42.5 0.0 all-gather.5.cloned.1.call-update
  42.5 0.0 all-gather.7.cloned.1.call-start
  42.6 0.8 reshape.96
  43.3 1.3 dynamic-slice
  45.3 0.3 dynamic-update-slice
  45.6 282.8 %all-reduce = s32[6144]{0:T(1024)S(1)} all-reduce(s32[6144]{0:T(1024)S(1)} %dynamic-update-slice), channel_id=1, replica_groups=mesh['sub'=64,'crow'=4,'ccol'=2] {'sub'}, use_global_device_ids=true, to_apply=%add | all-reduce | flops 6144 | bytes 49152
  328.4 0.0 all-gather.5.cloned.1.call-done
  328.4 16.2 %scatter_custom_fusion = bf16[769,128]{1,0:T(8,128)(2,1)S(1)} fusion(s32[6144]{0:T(1024)S(1)} %compare_select_fusion, bf16[6144,128]{1,0:T(8,128)(2,1)} %all-gather.5.cloned.1.call-done, bf16[]{:T(256)} %constant.10.clone.1), kind=kCustom, calls=%fused_computation.46 | custom fusion | bytes 197376 | tf_op jit(solution)/shard_map/scatter | solution.py:64
  344.6 1.1 convolution_bitcast_fusion.3
  345.7 30.7 %psum.43 = bf16[96,128]{1,0:T(8,128)(2,1)} all-reduce(f32[96,128]{1,0:T(8,128)S(1)} %convolution_bitcast_fusion.3), channel_id=1, replica_groups=mesh['sub'=64,'crow'=4,'ccol'=2] {'crow','ccol'}, use_global_device_ids=true, to_apply=%region_2.3 | all-reduce | flops 12288 | bytes 73728 | tf_op jit(solution)/shard_map/psum | solution.py:67
  376.4 0.0 all-gather.7.cloned.1.call-update
  376.4 0.0 all-reduce.4.cloned.1.call-start
  376.4 0.8 reshape.58
  377.2 75.1 %all-gather.7.cloned.1.call-done = bf16[6144,128]{1,0:T(8,128)(2,1)} async-done(((bf16[96,128]{1,0:T(8,128)(2,1)}), bf16[6144,128]{1,0:T(8,128)(2,1)}) %all-gather.7.cloned.1.call-update) | async-done | bytes 1572880 | tf_op jit(solution)/shard_map/all_gather | solution.py:68
  452.4 2.2 gather_fusion
  454.6 0.9 convolution_bitcast_fusion
  455.6 0.3 fusion.64
  455.9 27.2 %all_gather.28 = bf16[2,1024,128]{2,1,0:T(8,128)(2,1)S(1)} all-gather(bf16[2,128,128]{2,1,0:T(8,128)(2,1)S(1)} %get-tuple-element.6), channel_id=1, replica_groups=mesh['sub'=64,'crow'=4,'ccol'=2] {'crow','ccol'}, dimensions={1}, use_global_device_ids=true | all-gather | bytes 589824 | tf_op jit(solution)/shard_map/all_gather | solution.py:28
  483.1 0.3 convolution_convert_fusion.1
  483.4 0.3 fusion.8
  483.7 0.3 fusion.7
  484.0 0.7 pad_maximum_fusion
  484.6 0.0 all-reduce.4.cloned.1.call-update
  484.7 0.0 all-gather.9.cloned.1.call-start
  484.7 65.4 %all-reduce.4.cloned.1.call-done = bf16[2,2,128,128]{3,2,0,1:T(8,128)(2,1)} async-done(((bf16[2,2,128,128]{3,2,0,1:T(8,128)(2,1)}), bf16[2,2,128,128]{3,2,0,1:T(8,128)(2,1)}) %all-reduce.4.cloned.1.call-update) | async-done | bytes 131088 | tf_op jit(solution)/shard_map/psum | solution.py:35
  550.1 0.9 fusion.63
  550.9 8.1 collective-permute-start.1
  559.1 1.9 collective-permute-start
  561.0 0.2 collective-permute-done.1
  561.2 1.0 fusion.14
  562.2 6.5 collective-permute-done
  568.6 1.0 fusion.6
  569.6 0.1 convolution_bitcast_fusion.2
  569.8 30.8 %psum.45 = bf16[2,48,128]{2,1,0:T(8,128)(2,1)} all-reduce(f32[2,48,128]{2,1,0:T(8,128)S(1)} %convolution_bitcast_fusion.2), channel_id=1, replica_groups=mesh['sub'=64,'crow'=4,'ccol'=2] {'crow','ccol'}, use_global_device_ids=true, to_apply=%region_4.5 | all-reduce | flops 12288 | bytes 73728 | tf_op jit(solution)/shard_map/psum | solution.py:77
  600.6 0.0 all-gather.9.cloned.1.call-update
  600.6 0.0 all-gather.11.cloned.1.call-start
  600.7 77.5 %all-gather.9.cloned.1.call-done = bf16[6144,128]{1,0:T(8,128)(2,1)} async-done(((bf16[96,128]{1,0:T(8,128)(2,1)}), bf16[6144,128]{1,0:T(8,128)(2,1)}) %all-gather.9.cloned.1.call-update) | async-done | bytes 1572880 | tf_op jit(solution)/shard_map/all_gather | solution.py:55
  678.2 16.2 %scatter_custom_fusion.1 = bf16[769,128]{1,0:T(8,128)(2,1)S(1)} fusion(s32[6144]{0:T(1024)S(1)} %compare_select_fusion, bf16[6144,128]{1,0:T(8,128)(2,1)} %all-gather.9.cloned.1.call-done, bf16[]{:T(256)} %constant.10.clone.1), kind=kCustom, calls=%fused_computation.44 | custom fusion | bytes 197376 | tf_op jit(solution)/shard_map/scatter | solution.py:64
  694.4 0.2 convolution_bitcast_fusion.1
  694.6 30.9 %psum.46 = bf16[96,128]{1,0:T(8,128)(2,1)} all-reduce(f32[96,128]{1,0:T(8,128)S(1)} %convolution_bitcast_fusion.1), channel_id=1, replica_groups=mesh['sub'=64,'crow'=4,'ccol'=2] {'crow','ccol'}, use_global_device_ids=true, to_apply=%region_6.7 | all-reduce | flops 12288 | bytes 73728 | tf_op jit(solution)/shard_map/psum | solution.py:67
  725.5 0.0 all-gather.11.cloned.1.call-update
  725.5 0.0 all-reduce.6.cloned.1.call-start
  725.6 27.3 %all_gather.29 = bf16[2,1024,128]{2,1,0:T(8,128)(2,1)S(1)} all-gather(bf16[2,128,128]{2,1,0:T(8,128)(2,1)S(1)} %fusion.6), channel_id=1, replica_groups=mesh['sub'=64,'crow'=4,'ccol'=2] {'crow','ccol'}, dimensions={1}, use_global_device_ids=true | all-gather | bytes 589824 | tf_op jit(solution)/shard_map/all_gather | solution.py:108
  752.8 52.2 %all-gather.11.cloned.1.call-done = bf16[6144,128]{1,0:T(8,128)(2,1)} async-done(((bf16[96,128]{1,0:T(8,128)(2,1)}), bf16[6144,128]{1,0:T(8,128)(2,1)}) %all-gather.11.cloned.1.call-update) | async-done | bytes 1572880 | tf_op jit(solution)/shard_map/all_gather | solution.py:68
  805.1 2.2 gather_fusion.1
  807.3 0.2 fusion.66
  807.5 1.0 fusion.65
  808.5 27.2 %all_gather.32 = bf16[2,1024,128]{2,1,0:T(8,128)(2,1)S(1)} all-gather(bf16[2,128,128]{2,1,0:T(8,128)(2,1)S(1)} %get-tuple-element.8), channel_id=1, replica_groups=mesh['sub'=64,'crow'=4,'ccol'=2] {'crow','ccol'}, dimensions={1}, use_global_device_ids=true | all-gather | bytes 589824 | tf_op jit(solution)/shard_map/all_gather | solution.py:28
  835.7 0.3 convolution_convert_fusion
  836.0 0.3 fusion.10
  836.2 0.3 fusion.9
  836.5 0.7 pad_maximum_fusion.1
  837.2 0.0 all-reduce.6.cloned.1.call-update
  837.2 65.4 %all-reduce.6.cloned.1.call-done = bf16[2,2,128,128]{3,2,0,1:T(8,128)(2,1)} async-done(((bf16[2,2,128,128]{3,2,0,1:T(8,128)(2,1)}), bf16[2,2,128,128]{3,2,0,1:T(8,128)(2,1)}) %all-reduce.6.cloned.1.call-update) | async-done | bytes 131088 | tf_op jit(solution)/shard_map/psum | solution.py:35
  902.6 0.9 fusion.62
  903.5 8.1 collective-permute-start.3
  911.6 1.9 collective-permute-start.2
  913.6 0.2 collective-permute-done.3
  913.8 1.0 fusion.11
  914.7 6.5 collective-permute-done.2
  921.2 1.6 fusion.3
  (19 shorter events, 0.1 us)
Async XLA Ops:
  7.2 448.4 %copy-start = (bf16[2,128,1024]{2,1,0:T(8,128)(2,1)S(1)}, bf16[2,128,1024]{2,1,0:T(8,128)(2,1)}, u32[]{:S(2)}) copy-start(bf16[2,128,1024]{2,1,0:T(8,128)(2,1)} %param.10) | copy-start | bytes 1572868
  7.2 448.4 %copy-start.2 = (bf16[2,1024,128]{2,1,0:T(8,128)(2,1)S(1)}, bf16[2,1024,128]{2,1,0:T(8,128)(2,1)}, u32[]{:S(2)}) copy-start(bf16[2,1024,128]{2,1,0:T(8,128)(2,1)} %param.8) | copy-start | bytes 1572868
  7.2 321.2 %all-gather.5.cloned.1.call-start = ((), (), s32[]{:S(2)}) async-start(), calls=%async_computation | async-start | bytes 1597440 | tf_op jit(solution)/shard_map/all_gather | solution.py:55
  42.5 409.8 %all-gather.7.cloned.1.call-start = ((), (), s32[]{:S(2)}) async-start(), calls=%async_computation.1 | async-start | bytes 1597440 | tf_op jit(solution)/shard_map/all_gather | solution.py:68
  328.3 154.7 %copy-start.1 = (bf16[2,128,1024]{2,1,0:T(8,128)(2,1)S(1)}, bf16[2,128,1024]{2,1,0:T(8,128)(2,1)}, u32[]{:S(2)}) copy-start(bf16[2,128,1024]{2,1,0:T(8,128)(2,1)} %param.9) | copy-start | bytes 1572868
  376.4 173.7 %all-reduce.4.cloned.1.call-start = ((), (), s32[]{:S(2)}) async-start(), calls=%async_computation.2 | async-start | bytes 262144 | tf_op jit(solution)/shard_map/psum | solution.py:35
  455.6 27.8 %copy-start.5 = (s32[2,128]{1,0:T(2,128)S(1)}, s32[2,128]{1,0:T(2,128)}, u32[]{:S(2)}) copy-start(s32[2,128]{1,0:T(2,128)} %param.15) | copy-start | bytes 3076
  455.6 28.1 %copy-start.6 = (s32[2,128]{1,0:T(2,128)S(1)}, s32[2,128]{1,0:T(2,128)}, u32[]{:S(2)}) copy-start(s32[2,128]{1,0:T(2,128)} %param.14) | copy-start | bytes 3076
  483.1 86.6 %copy-start.4 = (bf16[2,128,48]{1,2,0:T(8,128)(2,1)S(1)}, bf16[2,128,48]{1,2,0:T(8,128)(2,1)}, u32[]{:S(2)}) copy-start(bf16[2,128,48]{1,2,0:T(8,128)(2,1)} %param.11) | copy-start | bytes 73732
  483.1 211.3 %copy-start.3 = (bf16[96,768]{1,0:T(8,128)(2,1)S(1)}, bf16[96,768]{1,0:T(8,128)(2,1)}, u32[]{:S(2)}) copy-start(bf16[96,768]{1,0:T(8,128)(2,1)} %param.12) | copy-start | bytes 442372
  484.7 193.5 %all-gather.9.cloned.1.call-start = ((), (), s32[]{:S(2)}) async-start(), calls=%async_computation.3 | async-start | bytes 1597440 | tf_op jit(solution)/shard_map/all_gather | solution.py:55
  550.9 10.3 %collective-permute-start.1 = (bf16[1,2,128,128]{3,2,0,1:T(8,128)(2,1)S(1)}, bf16[1,2,128,128]{3,2,0,1:T(8,128)(2,1)S(1)}, u32[]{:S(2)}, u32[]{:S(2)}) collective-permute-start(bf16[1,2,128,128]{3,2,0,1:T(8,128)(2,1)S(1)} %get-tuple-element.5), channel_id=1, source_target_pairs={{8,0},{16,8},{24,16},{32,24},{40,32},{48,40},{56,48},{64,56},{72,6... | collective-permute-start | bytes 196616 | tf_op jit(solution)/shard_map/ppermute | solution.py:16
  559.1 9.6 %collective-permute-start = (bf16[1,2,128,128]{3,2,0,1:T(8,128)(2,1)S(1)}, bf16[1,2,128,128]{3,2,0,1:T(8,128)(2,1)S(1)}, u32[]{:S(2)}, u32[]{:S(2)}) collective-permute-start(bf16[1,2,128,128]{3,2,0,1:T(8,128)(2,1)S(1)} %get-tuple-element.4), channel_id=1, source_target_pairs={{0,8},{8,16},{16,24},{24,32},{32,40},{40,48},{48,56},{56,64},{64,7... | collective-permute-start | bytes 196616 | tf_op jit(solution)/shard_map/ppermute | solution.py:13
  600.6 204.4 %all-gather.11.cloned.1.call-start = ((), (), s32[]{:S(2)}) async-start(), calls=%async_computation.4 | async-start | bytes 1597440 | tf_op jit(solution)/shard_map/all_gather | solution.py:68
  725.5 177.1 %all-reduce.6.cloned.1.call-start = ((), (), s32[]{:S(2)}) async-start(), calls=%async_computation.5 | async-start | bytes 262144 | tf_op jit(solution)/shard_map/psum | solution.py:35
  903.5 10.3 %collective-permute-start.3 = (bf16[1,2,128,128]{3,2,0,1:T(8,128)(2,1)S(1)}, bf16[1,2,128,128]{3,2,0,1:T(8,128)(2,1)S(1)}, u32[]{:S(2)}, u32[]{:S(2)}) collective-permute-start(bf16[1,2,128,128]{3,2,0,1:T(8,128)(2,1)S(1)} %get-tuple-element.3), channel_id=1, source_target_pairs={{8,0},{16,8},{24,16},{32,24},{40,32},{48,40},{56,48},{64,56},{72,6... | collective-permute-start | bytes 196616 | tf_op jit(solution)/shard_map/ppermute | solution.py:16
  911.6 9.6 %collective-permute-start.2 = (bf16[1,2,128,128]{3,2,0,1:T(8,128)(2,1)S(1)}, bf16[1,2,128,128]{3,2,0,1:T(8,128)(2,1)S(1)}, u32[]{:S(2)}, u32[]{:S(2)}) collective-permute-start(bf16[1,2,128,128]{3,2,0,1:T(8,128)(2,1)S(1)} %get-tuple-element.2), channel_id=1, source_target_pairs={{0,8},{8,16},{16,24},{24,32},{32,40},{40,48},{48,56},{56,64},{64,7... | collective-permute-start | bytes 196616 | tf_op jit(solution)/shard_map/ppermute | solution.py:13
Sparse Core Ops, SparseCore 0:
  42.7 83.8 all-gather.4
  376.5 75.8 all-gather.6
  484.8 65.2 all-reduce.3
  600.8 77.3 all-gather.8
  725.6 79.3 all-gather.10
  837.3 65.2 all-reduce.5
where the time goes:
time: 931 us; the launch traced here: 930 us
  blocking collectives  491 us (53%)
  waiting for transfers between devices  349 us (37%)
  local copies, waits for them, and re-layouts  41.7 us (4%)
  starting transfers between devices  20.3 us (2%)
  between operations  15 us (2%)
  matrix products  11.1 us (1%)
    unnamed x1, blocking collectives  283 us
    psum x2, waiting for transfers between devices, apply_stiffness(): boundary = lax.psum(partial_faces.astype(jnp.bfloat16), ('crow', 'ccol'))  131 us
    all_gather x2, waiting for transfers between devices, coarse_step(): everything = lax.all_gather(coarse, 'sub', axis=0, tiled=True)  127 us
    all_gather x2, waiting for transfers between devices, coarse_step(): lax.all_gather(flat_rows, 'sub', axis=0, tiled=True)  77.5 us
    psum x2, blocking collectives, precondition(): restricted = lax.psum(partial_modes, ('crow', 'ccol')).astype(jnp.bfloat16)  65 us
    psum x2, blocking collectives, coarse_step(): coarse = lax.psum(partial_coarse, ('crow', 'ccol')).astype(jnp.bfloat16)  61.6 us
    all_gather x2, blocking collectives, apply_stiffness(): lax.all_gather(rounded, ('crow', 'ccol'), axis=1, tiled=True)  54.3 us
    scatter x2, local copies, waits for them, and re-layouts, coarse_step(): ordered = jnp.zeros((block_width + 1, case_count), jnp.bfloat16).at[arriv...  32.4 us
  transfers between devices with their start and end apart: 10, of which 9 were waited for; matrix products, arithmetic and copies ran while one was open for 1% of the time, Pallas kernels for 0%

commit v1 on v0

--- a/solution.py
+++ b/solution.py
@@ -2,6 +2,12 @@
 import jax.numpy as jnp
 from jax import lax
 from jax.sharding import PartitionSpec as P
+
+
+def summed_here(shard, mesh_axis):
+    parts = lax.all_gather(shard, mesh_axis, axis=0, tiled=False)
+    total = parts.sum(axis=0)
+    return total
 
 
 def padded(block, sides, width):
@@ -32,7 +38,7 @@
         "sfi,sic->sfc", pick_right, product_b, preferred_element_type=jnp.float32
     )
     partial_faces = jnp.stack([left_part, right_part], axis=1)
-    boundary = lax.psum(partial_faces.astype(jnp.bfloat16), ("crow", "ccol"))
+    boundary = summed_here(partial_faces.astype(jnp.bfloat16), ("crow", "ccol"))
     extended = padded(boundary, (("sub", 0),), 1)
     from_before = extended[:sub_count, 1]
     from_after = extended[2:, 0]

time: 931 us -> 879 us (0.944)
  waiting for transfers between devices: 349 us -> 298 us
    psum x2 -> x0, waiting for transfers between devices: 131 us -> none  [apply_stiffness(): boundary = lax.psum(partial_faces.astype(jnp.bfloat16), ('crow', 'ccol'))]
    all_gather x0 -> x2, waiting for transfers between devices: none -> 78.4 us  [summed_here(): parts = lax.all_gather(shard, mesh_axis, axis=0, tiled=False)]
  transfers between devices with their start and end apart: 10 -> 10, of which waited for: 9 -> 9; matrix products, arithmetic and copies ran while one was open for 1% -> 0% of each run, Pallas kernels for 0% -> 0%
where the time goes in v1:
time: 879 us; the launch traced here: 876 us
  blocking collectives  492 us (56%)
  waiting for transfers between devices  298 us (34%)
  local copies, waits for them, and re-layouts  41.3 us (5%)
  starting transfers between devices  19.2 us (2%)
  between operations  15 us (2%)
    unnamed x1, blocking collectives  283 us
    all_gather x2, waiting for transfers between devices, coarse_step(): everything = lax.all_gather(coarse, 'sub', axis=0, tiled=True)  127 us
    all_gather x2, waiting for transfers between devices, summed_here(): parts = lax.all_gather(shard, mesh_axis, axis=0, tiled=False)  78.4 us
    all_gather x2, waiting for transfers between devices, coarse_step(): lax.all_gather(flat_rows, 'sub', axis=0, tiled=True)  77 us
    psum x2, blocking collectives, precondition(): restricted = lax.psum(partial_modes, ('crow', 'ccol')).astype(jnp.bfloat16)  66.3 us
    psum x2, blocking collectives, coarse_step(): coarse = lax.psum(partial_coarse, ('crow', 'ccol')).astype(jnp.bfloat16)  61.6 us
    all_gather x2, blocking collectives, apply_stiffness(): lax.all_gather(rounded, ('crow', 'ccol'), axis=1, tiled=True)  54.3 us
    scatter x2, local copies, waits for them, and re-layouts, coarse_step(): ordered = jnp.zeros((block_width + 1, case_count), jnp.bfloat16).at[arriv...  32.4 us
  transfers between devices with their start and end apart: 10, of which 9 were waited for; matrix products, arithmetic and copies ran while one was open for 0% of the time, Pallas kernels for 0%

profile of v1, /device:TPU:6, one launch (start us, length us, event | category | flops | bytes accessed | tf_op | source)
XLA Modules:
  0.0 876.4 jit_solution(8212281979953833809)
XLA Ops:
  7.2 0.0 all-gather.7.cloned.1.call-start
  7.2 1.1 convolution_bitcast_fusion.4
  8.3 34.2 %psum.28 = bf16[2,48,128]{2,1,0:T(8,128)(2,1)} all-reduce(f32[2,48,128]{2,1,0:T(8,128)S(1)} %convolution_bitcast_fusion.4), channel_id=1, replica_groups=mesh['sub'=64,'crow'=4,'ccol'=2] {'crow','ccol'}, use_global_device_ids=true, to_apply=%region_0.0 | all-reduce | flops 12288 | bytes 73728 | tf_op jit(solution)/shard_map/psum | solution.py:83
  42.5 0.0 all-gather.7.cloned.1.call-update
  42.5 0.0 all-gather.9.cloned.1.call-start
  42.6 0.8 reshape.162
  43.3 1.3 dynamic-slice
  45.3 0.3 dynamic-update-slice
  45.6 282.8 %all-reduce = s32[6144]{0:T(1024)S(1)} all-reduce(s32[6144]{0:T(1024)S(1)} %dynamic-update-slice), channel_id=1, replica_groups=mesh['sub'=64,'crow'=4,'ccol'=2] {'sub'}, use_global_device_ids=true, to_apply=%add | all-reduce | flops 6144 | bytes 49152
  328.4 0.0 all-gather.7.cloned.1.call-done
  328.4 16.2 %scatter_custom_fusion = bf16[769,128]{1,0:T(8,128)(2,1)S(1)} fusion(s32[6144]{0:T(1024)S(1)} %compare_select_fusion, bf16[6144,128]{1,0:T(8,128)(2,1)} %all-gather.7.cloned.1.call-done, bf16[]{:T(256)} %constant.10.clone.1), kind=kCustom, calls=%fused_computation.46 | custom fusion | bytes 197376 | tf_op jit(solution)/shard_map/scatter | solution.py:70
  344.6 1.1 convolution_bitcast_fusion.3
  345.7 30.7 %psum.29 = bf16[96,128]{1,0:T(8,128)(2,1)} all-reduce(f32[96,128]{1,0:T(8,128)S(1)} %convolution_bitcast_fusion.3), channel_id=1, replica_groups=mesh['sub'=64,'crow'=4,'ccol'=2] {'crow','ccol'}, use_global_device_ids=true, to_apply=%region_2.3 | all-reduce | flops 12288 | bytes 73728 | tf_op jit(solution)/shard_map/psum | solution.py:73
  376.4 0.0 all-gather.9.cloned.1.call-update
  376.4 0.0 all-gather.11.cloned.1.call-start
  376.4 0.8 reshape.124
  377.2 75.1 %all-gather.9.cloned.1.call-done = bf16[6144,128]{1,0:T(8,128)(2,1)} async-done(((bf16[96,128]{1,0:T(8,128)(2,1)}), bf16[6144,128]{1,0:T(8,128)(2,1)}) %all-gather.9.cloned.1.call-update) | async-done | bytes 1572880 | tf_op jit(solution)/shard_map/all_gather | solution.py:74
  452.4 2.2 gather_fusion
  454.6 0.9 convolution_bitcast_fusion
  455.6 0.3 fusion.64
  455.9 27.2 %all_gather.36 = bf16[2,1024,128]{2,1,0:T(8,128)(2,1)S(1)} all-gather(bf16[2,128,128]{2,1,0:T(8,128)(2,1)S(1)} %get-tuple-element.6), channel_id=1, replica_groups=mesh['sub'=64,'crow'=4,'ccol'=2] {'crow','ccol'}, dimensions={1}, use_global_device_ids=true | all-gather | bytes 589824 | tf_op jit(solution)/shard_map/all_gather | solution.py:34
  483.1 0.3 convolution_convert_fusion.1
  483.4 0.3 fusion.8
  483.7 0.3 fusion.7
  484.0 0.7 copy.51
  484.7 0.0 all-gather.11.cloned.1.call-update
  484.7 0.0 all-gather.13.cloned.1.call-start
  484.7 39.2 %all-gather.11.cloned.1.call-done = bf16[8,2,2,128,128]{4,3,2,1,0:T(8,128)(2,1)} async-done(((bf16[1,2,2,128,128]{4,3,2,1,0:T(8,128)(2,1)}), bf16[8,2,2,128,128]{4,3,2,1,0:T(8,128)(2,1)}) %all-gather.11.cloned.1.call-update) | async-done | bytes 1048592 | tf_op jit(solution)/shard_map/all_gather | solution.py:8
  523.9 1.4 reduce_sum.24
  525.3 7.6 collective-permute-start.1
  532.9 1.9 collective-permute-start
  534.8 0.1 collective-permute-done.1
  535.0 0.2 fusion.14
  535.2 7.2 collective-permute-done
  542.4 0.2 fusion.6
  542.6 0.1 convolution_bitcast_fusion.2
  542.8 32.1 %psum.30 = bf16[2,48,128]{2,1,0:T(8,128)(2,1)} all-reduce(f32[2,48,128]{2,1,0:T(8,128)S(1)} %convolution_bitcast_fusion.2), channel_id=1, replica_groups=mesh['sub'=64,'crow'=4,'ccol'=2] {'crow','ccol'}, use_global_device_ids=true, to_apply=%region_4.5 | all-reduce | flops 12288 | bytes 73728 | tf_op jit(solution)/shard_map/psum | solution.py:83
  574.8 0.0 all-gather.13.cloned.1.call-update
  574.9 0.0 all-gather.15.cloned.1.call-start
  574.9 77.0 %all-gather.13.cloned.1.call-done = bf16[6144,128]{1,0:T(8,128)(2,1)} async-done(((bf16[96,128]{1,0:T(8,128)(2,1)}), bf16[6144,128]{1,0:T(8,128)(2,1)}) %all-gather.13.cloned.1.call-update) | async-done | bytes 1572880 | tf_op jit(solution)/shard_map/all_gather | solution.py:61
  651.9 16.2 %scatter_custom_fusion.1 = bf16[769,128]{1,0:T(8,128)(2,1)S(1)} fusion(s32[6144]{0:T(1024)S(1)} %compare_select_fusion, bf16[6144,128]{1,0:T(8,128)(2,1)} %all-gather.13.cloned.1.call-done, bf16[]{:T(256)} %constant.10.clone.1), kind=kCustom, calls=%fused_computation.44 | custom fusion | bytes 197376 | tf_op jit(solution)/shard_map/scatter | solution.py:70
  668.1 0.2 convolution_bitcast_fusion.1
  668.3 30.9 %psum.31 = bf16[96,128]{1,0:T(8,128)(2,1)} all-reduce(f32[96,128]{1,0:T(8,128)S(1)} %convolution_bitcast_fusion.1), channel_id=1, replica_groups=mesh['sub'=64,'crow'=4,'ccol'=2] {'crow','ccol'}, use_global_device_ids=true, to_apply=%region_6.7 | all-reduce | flops 12288 | bytes 73728 | tf_op jit(solution)/shard_map/psum | solution.py:73
  699.2 0.0 all-gather.15.cloned.1.call-update
  699.2 0.0 all-gather.17.cloned.1.call-start
  699.3 27.3 %all_gather.38 = bf16[2,1024,128]{2,1,0:T(8,128)(2,1)S(1)} all-gather(bf16[2,128,128]{2,1,0:T(8,128)(2,1)S(1)} %fusion.6), channel_id=1, replica_groups=mesh['sub'=64,'crow'=4,'ccol'=2] {'crow','ccol'}, dimensions={1}, use_global_device_ids=true | all-gather | bytes 589824 | tf_op jit(solution)/shard_map/all_gather | solution.py:114
  726.6 52.2 %all-gather.15.cloned.1.call-done = bf16[6144,128]{1,0:T(8,128)(2,1)} async-done(((bf16[96,128]{1,0:T(8,128)(2,1)}), bf16[6144,128]{1,0:T(8,128)(2,1)}) %all-gather.15.cloned.1.call-update) | async-done | bytes 1572880 | tf_op jit(solution)/shard_map/all_gather | solution.py:74
  778.8 2.2 gather_fusion.1
  781.0 0.2 fusion.66
  781.2 1.0 fusion.65
  782.2 27.2 %all_gather.41 = bf16[2,1024,128]{2,1,0:T(8,128)(2,1)S(1)} all-gather(bf16[2,128,128]{2,1,0:T(8,128)(2,1)S(1)} %get-tuple-element.8), channel_id=1, replica_groups=mesh['sub'=64,'crow'=4,'ccol'=2] {'crow','ccol'}, dimensions={1}, use_global_device_ids=true | all-gather | bytes 589824 | tf_op jit(solution)/shard_map/all_gather | solution.py:34
  809.4 0.3 convolution_convert_fusion
  809.7 0.3 fusion.10
  809.9 0.3 fusion.9
  810.3 0.7 copy.65
  810.9 0.0 all-gather.17.cloned.1.call-update
  811.0 39.2 %all-gather.17.cloned.1.call-done = bf16[8,2,2,128,128]{4,3,2,1,0:T(8,128)(2,1)} async-done(((bf16[1,2,2,128,128]{4,3,2,1,0:T(8,128)(2,1)}), bf16[8,2,2,128,128]{4,3,2,1,0:T(8,128)(2,1)}) %all-gather.17.cloned.1.call-update) | async-done | bytes 1048592 | tf_op jit(solution)/shard_map/all_gather | solution.py:8
  850.2 1.4 reduce_sum.25
  851.6 7.6 collective-permute-start.3
  859.2 1.9 collective-permute-start.2
  861.1 0.1 collective-permute-done.3
  861.2 0.2 fusion.11
  861.4 7.2 collective-permute-done.2
  868.7 0.9 fusion.3
  (23 shorter events, 0.1 us)
Async XLA Ops:
  7.2 448.4 %copy-start = (bf16[2,128,1024]{2,1,0:T(8,128)(2,1)S(1)}, bf16[2,128,1024]{2,1,0:T(8,128)(2,1)}, u32[]{:S(2)}) copy-start(bf16[2,128,1024]{2,1,0:T(8,128)(2,1)} %param.10) | copy-start | bytes 1572868
  7.2 448.4 %copy-start.2 = (bf16[2,1024,128]{2,1,0:T(8,128)(2,1)S(1)}, bf16[2,1024,128]{2,1,0:T(8,128)(2,1)}, u32[]{:S(2)}) copy-start(bf16[2,1024,128]{2,1,0:T(8,128)(2,1)} %param.8) | copy-start | bytes 1572868
  7.2 321.2 %all-gather.7.cloned.1.call-start = ((), (), s32[]{:S(2)}) async-start(), calls=%async_computation | async-start | bytes 1597440 | tf_op jit(solution)/shard_map/all_gather | solution.py:61
  42.5 409.8 %all-gather.9.cloned.1.call-start = ((), (), s32[]{:S(2)}) async-start(), calls=%async_computation.1 | async-start | bytes 1597440 | tf_op jit(solution)/shard_map/all_gather | solution.py:74
  328.3 154.7 %copy-start.1 = (bf16[2,128,1024]{2,1,0:T(8,128)(2,1)S(1)}, bf16[2,128,1024]{2,1,0:T(8,128)(2,1)}, u32[]{:S(2)}) copy-start(bf16[2,128,1024]{2,1,0:T(8,128)(2,1)} %param.9) | copy-start | bytes 1572868
  376.4 147.5 %all-gather.11.cloned.1.call-start = ((), (), s32[]{:S(2)}) async-start(), calls=%async_computation.2 | async-start | bytes 1179648 | tf_op jit(solution)/shard_map/all_gather | solution.py:8
  455.6 27.8 %copy-start.5 = (s32[2,128]{1,0:T(2,128)S(1)}, s32[2,128]{1,0:T(2,128)}, u32[]{:S(2)}) copy-start(s32[2,128]{1,0:T(2,128)} %param.15) | copy-start | bytes 3076
  455.6 28.1 %copy-start.6 = (s32[2,128]{1,0:T(2,128)S(1)}, s32[2,128]{1,0:T(2,128)}, u32[]{:S(2)}) copy-start(s32[2,128]{1,0:T(2,128)} %param.14) | copy-start | bytes 3076
  483.4 59.3 %copy-start.4 = (bf16[2,128,48]{1,2,0:T(8,128)(2,1)S(1)}, bf16[2,128,48]{1,2,0:T(8,128)(2,1)}, u32[]{:S(2)}) copy-start(bf16[2,128,48]{1,2,0:T(8,128)(2,1)} %param.11) | copy-start | bytes 73732
  484.0 184.1 %copy-start.3 = (bf16[96,768]{1,0:T(8,128)(2,1)S(1)}, bf16[96,768]{1,0:T(8,128)(2,1)}, u32[]{:S(2)}) copy-start(bf16[96,768]{1,0:T(8,128)(2,1)} %param.12) | copy-start | bytes 442372
  484.7 167.2 %all-gather.13.cloned.1.call-start = ((), (), s32[]{:S(2)}) async-start(), calls=%async_computation.3 | async-start | bytes 1597440 | tf_op jit(solution)/shard_map/all_gather | solution.py:61
  525.3 9.6 %collective-permute-start.1 = (bf16[1,2,128,128]{3,2,0,1:T(8,128)(2,1)S(1)}, bf16[1,2,128,128]{3,2,0,1:T(8,128)(2,1)S(1)}, u32[]{:S(2)}, u32[]{:S(2)}) collective-permute-start(bf16[1,2,128,128]{3,2,0,1:T(8,128)(2,1)S(1)} %get-tuple-element.5), channel_id=1, source_target_pairs={{8,0},{16,8},{24,16},{32,24},{40,32},{48,40},{56,48},{64,56},{72,6... | collective-permute-start | bytes 196616 | tf_op jit(solution)/shard_map/ppermute | solution.py:22
  532.9 9.5 %collective-permute-start = (bf16[1,2,128,128]{3,2,0,1:T(8,128)(2,1)S(1)}, bf16[1,2,128,128]{3,2,0,1:T(8,128)(2,1)S(1)}, u32[]{:S(2)}, u32[]{:S(2)}) collective-permute-start(bf16[1,2,128,128]{3,2,0,1:T(8,128)(2,1)S(1)} %get-tuple-element.4), channel_id=1, source_target_pairs={{0,8},{8,16},{16,24},{24,32},{32,40},{40,48},{48,56},{56,64},{64,7... | collective-permute-start | bytes 196616 | tf_op jit(solution)/shard_map/ppermute | solution.py:19
  574.9 203.9 %all-gather.15.cloned.1.call-start = ((), (), s32[]{:S(2)}) async-start(), calls=%async_computation.4 | async-start | bytes 1597440 | tf_op jit(solution)/shard_map/all_gather | solution.py:74
  699.2 151.0 %all-gather.17.cloned.1.call-start = ((), (), s32[]{:S(2)}) async-start(), calls=%async_computation.5 | async-start | bytes 1179648 | tf_op jit(solution)/shard_map/all_gather | solution.py:8
  851.6 9.6 %collective-permute-start.3 = (bf16[1,2,128,128]{3,2,0,1:T(8,128)(2,1)S(1)}, bf16[1,2,128,128]{3,2,0,1:T(8,128)(2,1)S(1)}, u32[]{:S(2)}, u32[]{:S(2)}) collective-permute-start(bf16[1,2,128,128]{3,2,0,1:T(8,128)(2,1)S(1)} %get-tuple-element.3), channel_id=1, source_target_pairs={{8,0},{16,8},{24,16},{32,24},{40,32},{48,40},{56,48},{64,56},{72,6... | collective-permute-start | bytes 196616 | tf_op jit(solution)/shard_map/ppermute | solution.py:22
  859.2 9.5 %collective-permute-start.2 = (bf16[1,2,128,128]{3,2,0,1:T(8,128)(2,1)S(1)}, bf16[1,2,128,128]{3,2,0,1:T(8,128)(2,1)S(1)}, u32[]{:S(2)}, u32[]{:S(2)}) collective-permute-start(bf16[1,2,128,128]{3,2,0,1:T(8,128)(2,1)S(1)} %get-tuple-element.2), channel_id=1, source_target_pairs={{0,8},{8,16},{16,24},{24,32},{32,40},{40,48},{48,56},{56,64},{64,7... | collective-permute-start | bytes 196616 | tf_op jit(solution)/shard_map/ppermute | solution.py:19
Sparse Core Ops, SparseCore 0:
  42.7 83.8 all-gather.6
  376.5 75.8 all-gather.8
  484.8 39.0 all-gather.10
  575.0 76.8 all-gather.12
  699.3 79.3 all-gather.14
  811.1 39.0 all-gather.16
